TPU v7x, 32 devices: a whole 2x2x4 slice. The times are simulated.
32 devices in a mesh: tm: 4 (over z), space: 8 (over y, x, core).
Axes of the slice: x: 2, y: 2, z: 4, core: 2. Of those that a mesh axis runs over, the one named last changes fastest.
Arguments:
- positions: float32 [3, 8192], P(None, 'space'), may hold values from -6 to 6
- strengths: float32 [3, 8192], P(None, 'space'), may hold values from -6 to 6
- source_lists: int32 [64, 8], P('space'), may hold values from 0 to 63, as said below
- block_slot: int32 [64], replicated, may hold values from 0 to 63, as said below
Outputs:
- slice_ends: float32 [4, 6, 8192], P('tm', None, 'space')
Inputs may be any that keep to these rules, and one draw needn't show every extreme that they name: `source_lists`: the 8 ids of a row are distinct. Logical block g is stored as block block_slot[g], on space device block_slot[g] // 8. Among all entries of the 8 rows of one space device, at most 16 are stored on any one space device, and one space device, the same for all rows, holds exactly 16 of the entries of every space device. `block_slot`: A permutation of the logical block ids.
All inputs are finite; a program needn't handle non-finite values.
Results may differ from a plain program's by a relative error of at most 0.0003.
Values sent between devices are 32-bit elements; how exact they have to be, the bound alone decides.
A program may use at most 64 MiB of HBM per device.

v0:
```python
import functools

import jax
import jax.numpy as jnp
from jax import lax
from jax.experimental import pallas as pl
from jax.experimental.pallas import tpu as pltpu
from jax.sharding import PartitionSpec as P

BLOCK = 128
SUB = 8
PIECES = 6
MESH = pl.DeviceIdType.MESH

time_step = 0.1
core_square = 0.25
inv_four_pi = 0.07957747154594767


def cross(u, v):
    return [
        u[1] * v[2] - u[2] * v[1],
        u[2] * v[0] - u[0] * v[2],
        u[0] * v[1] - u[1] * v[0],
    ]


def dot3(u, v):
    return u[0] * v[0] + u[1] * v[1] + u[2] * v[2]


def rounded(v):
    return v.astype(jnp.bfloat16).astype(jnp.float32)


def split3(v):
    high = rounded(v)
    rest = v - high
    middle = rounded(rest)
    return high, middle, rounded(rest - middle)


def kernel(
    spaces, slices, blocks, width,
    pos_ref, str_ref, list_ref, slot_ref, out_ref,
    gathered, base, rate, f0, f1, f2, c0, incoming, outgoing,
    rows_a, rows_b, feat, moment, coef, send_sem, recv_sem, pass_sem,
):
    me = lax.axis_index("space")
    g = lax.axis_index("tm")
    h = time_step

    barrier = pltpu.get_barrier_semaphore()

    def greet(d, carry):
        peer = lax.rem(me + d, spaces)
        pl.semaphore_signal(barrier, inc=1, device_id={"space": peer}, device_id_type=MESH)
        return carry

    lax.fori_loop(1, spaces, greet, 0)

    @pl.when(g > 0)
    def _():
        pl.semaphore_signal(barrier, inc=1, device_id={"tm": g - 1}, device_id_type=MESH)

    @pl.when(g < slices - 1)
    def _():
        pl.semaphore_signal(barrier, inc=1, device_id={"tm": g + 1}, device_id_type=MESH)

    for b in range(blocks):
        cols = slice(b * BLOCK, (b + 1) * BLOCK)
        for r in range(3):
            gathered[0, me, r, b : b + 1, :] = pos_ref[r : r + 1, cols]
            gathered[0, me, 3 + r, b : b + 1, :] = str_ref[r : r + 1, cols]

    neighbours = jnp.where(g > 0, 1, 0) + jnp.where(g < slices - 1, 1, 0)
    pl.semaphore_wait(barrier, spaces - 1 + neighbours)

    def copy_to(slot, d):
        peer = lax.rem(me + d, spaces)
        return pltpu.make_async_remote_copy(
            src_ref=gathered.at[slot, me],
            dst_ref=gathered.at[slot, me],
            send_sem=send_sem.at[slot, d],
            recv_sem=recv_sem.at[slot, d],
            device_id={"space": peer},
            device_id_type=MESH,
        )

    def copy_from(slot, d):
        peer = lax.rem(me + spaces - d, spaces)
        return peer, pltpu.make_async_remote_copy(
            src_ref=gathered.at[slot, me],
            dst_ref=gathered.at[slot, peer],
            send_sem=send_sem.at[slot, d],
            recv_sem=recv_sem.at[slot, d],
            device_id={"space": peer},
            device_id_type=MESH,
        )

    def pass_copy():
        return pltpu.make_async_remote_copy(
            src_ref=outgoing,
            dst_ref=incoming,
            send_sem=pass_sem.at[0],
            recv_sem=pass_sem.at[1],
            device_id={"tm": lax.rem(g + 1, slices)},
            device_id_type=MESH,
        )

    def rows_of(ref, values):
        for r, v in enumerate(values):
            ref[pl.ds(r, blocks, stride=SUB), :] = v

    def source_features(slot, p):
        x = [gathered[slot, p, r] for r in range(3)]
        a = [gathered[slot, p, 3 + r] for r in range(3)]
        zero = jnp.zeros_like(x[0])
        rows_of(rows_a, x + a + [dot3(x, x), zero + 1.0])
        rows_of(rows_b, a + cross(x, a) + [zero, zero])
        high, middle, low = split3(rows_a[...].reshape(blocks, SUB, BLOCK))
        feat[pl.ds(p * blocks, blocks)] = jnp.concatenate(
            [high, high, high, middle, middle, low], 1
        ).astype(jnp.bfloat16)
        whole = rows_b[...].reshape(blocks, SUB, BLOCK)
        high = rounded(whole)
        moment[pl.ds(p * blocks, blocks)] = jnp.concatenate(
            [high, whole - high], 1
        ).astype(jnp.bfloat16)

    def target_features(slot):
        x = [gathered[slot, me, r] for r in range(3)]
        a = [gathered[slot, me, 3 + r] for r in range(3)]
        zero = jnp.zeros_like(x[0])
        rows_of(rows_a, [-2.0 * v for v in x] + [zero] * 3 + [zero + 1.0, dot3(x, x) + core_square])
        rows_of(rows_b, [-v for v in a] + [zero] * 4 + [dot3(a, x)])
        for half, ref in enumerate((rows_a, rows_b)):
            high, middle, low = split3(ref[...].reshape(blocks, SUB, BLOCK))
            coef[:, :, half * BLOCK : (half + 1) * BLOCK] = jnp.concatenate(
                [high, middle, low, high, middle, high], 1
            ).astype(jnp.bfloat16)

    def one_target(i, carry):
        left = coef[i]
        total = jnp.zeros((2 * SUB, 2 * BLOCK), jnp.float32)
        group = 2 if width % 2 == 0 else 1
        for j in range(0, width, group):
            at = [slot_ref[list_ref[i, j + k]] for k in range(group)]
            right = jnp.concatenate([feat[p] for p in at], 1)
            both = lax.dot_general(
                left, right, (((0,), (0,)), ((), ())), preferred_element_type=jnp.float32
            )
            inverse = lax.rsqrt(both[:BLOCK])
            square = inverse * inverse
            three = square * inverse
            five = three * (square * both[BLOCK:])
            weight = jnp.concatenate([three, five], 0)
            high = weight.astype(jnp.bfloat16)
            low = (weight - high.astype(jnp.float32)).astype(jnp.bfloat16)
            sums = jnp.concatenate([moment[p] for p in at], 1)
            for part in (high, low):
                total += lax.dot_general(
                    sums, part, (((1,), (1,)), ((), ())), preferred_element_type=jnp.float32
                )
        whole = total[:SUB] + total[SUB:]
        at_rows = pl.ds(pl.multiple_of(i * SUB, SUB), SUB)
        rows_a[at_rows, :] = whole[:, :BLOCK]
        rows_b[at_rows, :] = whole[:, BLOCK:]
        return carry

    def evaluate(slot):
        for d in range(1, spaces):
            copy_to(slot, d).start()
        target_features(slot)
        source_features(slot, me)

        def arrive(d, carry):
            peer, copy = copy_from(slot, d)
            copy.wait_recv()
            source_features(slot, peer)
            return carry

        lax.fori_loop(1, spaces, arrive, 0)
        lax.fori_loop(0, blocks, one_target, 0)
        x = [gathered[slot, me, r] for r in range(3)]
        a = [gathered[slot, me, 3 + r] for r in range(3)]
        pick = lambda ref, r: ref[pl.ds(r, blocks, stride=SUB), :]
        three_a = [pick(rows_a, r) for r in range(3)]
        three_b = [pick(rows_a, 3 + r) for r in range(3)]
        five_a = [pick(rows_b, r) for r in range(3)]
        five_b = [pick(rows_b, 3 + r) for r in range(3)]
        cross_v = cross(x, three_a)
        cross_s = cross(a, three_a)
        cross_f = cross(x, five_a)
        for r in range(3):
            rate[r] = -inv_four_pi * (cross_v[r] - three_b[r])
            rate[3 + r] = -inv_four_pi * (cross_s[r] - 3.0 * (cross_f[r] - five_b[r]))
        for d in range(1, spaces):
            copy_to(slot, d).wait_send()

    def write_out(value):
        for b in range(blocks):
            for r in range(6):
                out_ref[0, r : r + 1, b * BLOCK : (b + 1) * BLOCK] = value[r, b : b + 1, :]

    second = 3 + g
    steps = jnp.where(g == 0, 4, jnp.where(g < slices - 1, g + 8, g + 7))

    def step(s, carry):
        slot = lax.rem(s, 2)
        other = 1 - slot
        evaluate(slot)
        current = gathered[slot, me]
        now = rate[...]
        part = jnp.where(s < 4, s, s - second)

        @pl.when(part == 0)
        def _():
            base[...] = current
            f0[...] = now
            gathered[other, me] = current + (0.5 * h) * now

        @pl.when(part == 1)
        def _():
            f1[...] = now
            gathered[other, me] = current + (0.5 * h) * now

        @pl.when(part == 2)
        def _():
            f2[...] = now
            gathered[other, me] = base[...] + h * (
                5.0 / 24.0 * f0[...] + 1.0 / 3.0 * f1[...] - 1.0 / 24.0 * now
            )

        @pl.when(part == 3)
        def _():
            end = (
                current
                + (0.5 * h) * (now - f1[...])
                + h * (-1.0 / 24.0 * f0[...] + 1.0 / 3.0 * f1[...] + 5.0 / 24.0 * f2[...])
            )
            coarse = base[...] + h * f0[...]
            correction = end - coarse

            @pl.when(s == 3)
            def _():
                c0[...] = correction

            @pl.when((s > 3) & (g > 1))
            def _():
                pass_copy().wait_recv()
                gathered[other, me] = incoming[...] + correction

            @pl.when((s == 3) | (g <= 1))
            def _():
                gathered[other, me] = coarse + correction

            @pl.when((s > 3) | (g == 0))
            def _():
                write_out(gathered[other, me])

        @pl.when(part < 0)
        def _():
            gathered[other, me] = current + h * now + c0[...]

        @pl.when(part == 4)
        def _():
            outgoing[...] = current + h * now
            copy = pass_copy()
            copy.start()
            copy.wait_send()

        return carry

    lax.fori_loop(0, steps, step, 0)


def per_device(spaces, slices, positions, strengths, source_lists, block_slot):
    blocks, width = source_lists.shape
    whole = block_slot.shape[0]
    state = pltpu.VMEM((6, blocks, BLOCK), jnp.float32)
    vmem = pl.BlockSpec(memory_space=pltpu.VMEM)
    smem = pl.BlockSpec(memory_space=pltpu.SMEM)
    return pl.pallas_call(
        functools.partial(kernel, spaces, slices, blocks, width),
        out_shape=jax.ShapeDtypeStruct((1, 6, blocks * BLOCK), jnp.float32),
        in_specs=[vmem, vmem, smem, smem],
        out_specs=vmem,
        scratch_shapes=[
            pltpu.VMEM((2, spaces, 6, blocks, BLOCK), jnp.float32),
            state, state, state, state, state, state, state, state,
            pltpu.VMEM((blocks * SUB, BLOCK), jnp.float32),
            pltpu.VMEM((blocks * SUB, BLOCK), jnp.float32),
            pltpu.VMEM((whole, PIECES * SUB, BLOCK), jnp.bfloat16),
            pltpu.VMEM((whole, 2 * SUB, BLOCK), jnp.bfloat16),
            pltpu.VMEM((blocks, PIECES * SUB, 2 * BLOCK), jnp.bfloat16),
            pltpu.SemaphoreType.DMA((2, spaces)),
            pltpu.SemaphoreType.DMA((2, spaces)),
            pltpu.SemaphoreType.DMA((2,)),
        ],
        compiler_params=pltpu.CompilerParams(collective_id=0, has_side_effects=True),
    )(positions, strengths, source_lists, block_slot)


def solution(mesh):
    return jax.shard_map(
        functools.partial(per_device, mesh.shape["space"], mesh.shape["tm"]),
        mesh=mesh,
        in_specs=(P(None, "space"), P(None, "space"), P("space", None), P()),
        out_specs=P("tm", None, "space"),
        check_vma=False,
    )
```

profile of v0, /device:TPU:24, one launch (start us, length us, event | category | flops | bytes accessed | tf_op | source)
XLA Modules:
  0.0 124.1 jit_solution(16321293044561865640)
XLA Ops:
  0.0 122.7 %shard_map.46 = f32[1,6,1024]{2,1,0:T(8,128)} custom-call(f32[3,1024]{1,0:T(4,128)} %pos_ref.1, f32[3,1024]{1,0:T(4,128)} %str_ref.1, s32[8,8]{1,0:T(8,128)} %list_ref.1, s32[64]{0:T(128)} %slot_ref.1), custom_call_target="tpu_custom_call" | custom-call | tf_op jit(solution)/shard_map/pallas_call | solution.py:284
  122.7 1.4 %copy.5 = f32[1,6,1024]{2,0,1:T(1,128)} copy(f32[1,6,1024]{2,1,0:T(8,128)} %shard_map.46) | data formatting | bytes 49152 | tf_op jit(solution)/shard_map/pallas_call | solution.py:284
where the time goes:
time: 124 us
  Pallas kernels  123 us (99%)
  local copies, waits for them, and re-layouts  1.39 us (1%)
    pallas_call x1, Pallas kernels, per_device(): pl.pallas_call(functools.partial(kernel, spaces, slices, blocks, width),...  123 us

commit v1 on v0

--- a/solution.py
+++ b/solution.py
@@ -10,6 +10,8 @@
 BLOCK = 128
 SUB = 8
 PIECES = 6
+TOGETHER = 8
+AHEAD = 2
 MESH = pl.DeviceIdType.MESH
 
 time_step = 0.1
@@ -136,37 +138,61 @@
         rows_of(rows_b, [-v for v in a] + [zero] * 4 + [dot3(a, x)])
         for half, ref in enumerate((rows_a, rows_b)):
             high, middle, low = split3(ref[...].reshape(blocks, SUB, BLOCK))
-            coef[:, :, half * BLOCK : (half + 1) * BLOCK] = jnp.concatenate(
-                [high, middle, low, high, middle, high], 1
-            ).astype(jnp.bfloat16)
-
-    def one_target(i, carry):
-        left = coef[i]
-        total = jnp.zeros((2 * SUB, 2 * BLOCK), jnp.float32)
-        group = 2 if width % 2 == 0 else 1
-        for j in range(0, width, group):
-            at = [slot_ref[list_ref[i, j + k]] for k in range(group)]
-            right = jnp.concatenate([feat[p] for p in at], 1)
-            both = lax.dot_general(
-                left, right, (((0,), (0,)), ((), ())), preferred_element_type=jnp.float32
+            pieces = jnp.concatenate([high, middle, low, high, middle, high], 1)
+            for b in range(blocks):
+                coef[b, half * BLOCK : (half + 1) * BLOCK, :] = pieces[b].T.astype(jnp.bfloat16)
+
+    group = 2 if width % 2 == 0 else 1
+
+    def pair_product(i, j):
+        at = [slot_ref[list_ref[i, j + k]] for k in range(group)]
+        right = jnp.concatenate([feat[p] for p in at], 1)
+        both = lax.dot_general(
+            coef[i], right, (((1,), (0,)), ((), ())), preferred_element_type=jnp.float32
+        )
+        return at, both
+
+    def pair_sums(at, both):
+        inverse = lax.rsqrt(both[:BLOCK])
+        square = inverse * inverse
+        three = square * inverse
+        five = three * (square * both[BLOCK:])
+        weight = jnp.concatenate([three, five], 0)
+        high = weight.astype(jnp.bfloat16)
+        low = (weight - high.astype(jnp.float32)).astype(jnp.bfloat16)
+        sums = jnp.concatenate([moment[p] for p in at], 1)
+        total = 0.0
+        for part in (high, low):
+            total += lax.dot_general(
+                sums, part, (((1,), (1,)), ((), ())), preferred_element_type=jnp.float32
             )
-            inverse = lax.rsqrt(both[:BLOCK])
-            square = inverse * inverse
-            three = square * inverse
-            five = three * (square * both[BLOCK:])
-            weight = jnp.concatenate([three, five], 0)
-            high = weight.astype(jnp.bfloat16)
-            low = (weight - high.astype(jnp.float32)).astype(jnp.bfloat16)
-            sums = jnp.concatenate([moment[p] for p in at], 1)
-            for part in (high, low):
-                total += lax.dot_general(
-                    sums, part, (((1,), (1,)), ((), ())), preferred_element_type=jnp.float32
-                )
-        whole = total[:SUB] + total[SUB:]
-        at_rows = pl.ds(pl.multiple_of(i * SUB, SUB), SUB)
-        rows_a[at_rows, :] = whole[:, :BLOCK]
-        rows_b[at_rows, :] = whole[:, BLOCK:]
-        return carry
+        return total
+
+    def some_targets(first, count):
+        work = [(i, j) for i in range(count) for j in range(0, width, group)]
+        waiting = []
+        totals = [0.0] * count
+        for k in range(len(work) + AHEAD):
+            if k < len(work):
+                i, j = work[k]
+                waiting.append((i, pair_product(first + i, j)))
+            if k >= AHEAD:
+                i, (at, both) = waiting.pop(0)
+                totals[i] += pair_sums(at, both)
+                if k - AHEAD == len(work) - 1 or work[k - AHEAD + 1][0] != i:
+                    whole = totals[i][:SUB] + totals[i][SUB:]
+                    at_rows = pl.ds(pl.multiple_of((first + i) * SUB, SUB), SUB)
+                    rows_a[at_rows, :] = whole[:, :BLOCK]
+                    rows_b[at_rows, :] = whole[:, BLOCK:]
+
+    def all_targets():
+        per = TOGETHER if blocks % TOGETHER == 0 else 1
+
+        def body(k, carry):
+            some_targets(k * per, per)
+            return carry
+
+        lax.fori_loop(0, blocks // per, body, 0)
 
     def evaluate(slot):
         for d in range(1, spaces):
@@ -181,7 +207,7 @@
             return carry
 
         lax.fori_loop(1, spaces, arrive, 0)
-        lax.fori_loop(0, blocks, one_target, 0)
+        all_targets()
         x = [gathered[slot, me, r] for r in range(3)]
         a = [gathered[slot, me, 3 + r] for r in range(3)]
         pick = lambda ref, r: ref[pl.ds(r, blocks, stride=SUB), :]
@@ -293,7 +319,7 @@
             pltpu.VMEM((blocks * SUB, BLOCK), jnp.float32),
             pltpu.VMEM((whole, PIECES * SUB, BLOCK), jnp.bfloat16),
             pltpu.VMEM((whole, 2 * SUB, BLOCK), jnp.bfloat16),
-            pltpu.VMEM((blocks, PIECES * SUB, 2 * BLOCK), jnp.bfloat16),
+            pltpu.VMEM((blocks, 2 * BLOCK, PIECES * SUB), jnp.bfloat16),
             pltpu.SemaphoreType.DMA((2, spaces)),
             pltpu.SemaphoreType.DMA((2, spaces)),
             pltpu.SemaphoreType.DMA((2,)),

time: 124 us -> 85.5 us (0.69)
  Pallas kernels: 123 us -> 83.8 us
    pallas_call x1, Pallas kernels: 123 us -> 83.8 us  [per_device(): pl.pallas_call(functools.partial(kernel, spaces, slices, blocks, width),...]
where the time goes in v1:
time: 85.5 us; the launch traced here: 85.2 us
  Pallas kernels  83.8 us (98%)
  local copies, waits for them, and re-layouts  1.39 us (2%)
    pallas_call x1, Pallas kernels, per_device(): pl.pallas_call(functools.partial(kernel, spaces, slices, blocks, width),...  83.8 us

profile of v1, /device:TPU:24, one launch (start us, length us, event | category | flops | bytes accessed | tf_op | source)
XLA Modules:
  0.0 85.2 jit_solution(800222453971002276)
XLA Ops:
  0.0 83.8 %shard_map.46 = f32[1,6,1024]{2,1,0:T(8,128)} custom-call(f32[3,1024]{1,0:T(4,128)} %pos_ref.1, f32[3,1024]{1,0:T(4,128)} %str_ref.1, s32[8,8]{1,0:T(8,128)} %list_ref.1, s32[64]{0:T(128)} %slot_ref.1), custom_call_target="tpu_custom_call" | custom-call | tf_op jit(solution)/shard_map/pallas_call | solution.py:310
  83.9 1.4 %copy.5 = f32[1,6,1024]{2,0,1:T(1,128)} copy(f32[1,6,1024]{2,1,0:T(8,128)} %shard_map.46) | data formatting | bytes 49152 | tf_op jit(solution)/shard_map/pallas_call | solution.py:310

commit v2 on v1

--- a/solution.py
+++ b/solution.py
@@ -11,7 +11,7 @@
 SUB = 8
 PIECES = 6
 TOGETHER = 8
-AHEAD = 2
+AHEAD = 6
 MESH = pl.DeviceIdType.MESH
 
 time_step = 0.1
@@ -78,27 +78,37 @@
     neighbours = jnp.where(g > 0, 1, 0) + jnp.where(g < slices - 1, 1, 0)
     pl.semaphore_wait(barrier, spaces - 1 + neighbours)
 
-    def copy_to(slot, d):
-        peer = lax.rem(me + d, spaces)
+    chips = spaces // 2
+    tall = chips // 2
+    core = lax.rem(me, 2)
+    column = lax.rem(me // 2, 2)
+    row = me // 4
+    partner = me + 1 - 2 * core
+
+    def twin(d, sign):
+        other_column = lax.rem(column + d % 2, 2)
+        other_row = lax.rem(row + tall + sign * (d // 2), tall)
+        return 2 * (2 * other_row + other_column) + core
+
+    def copy(slot, what, where, sem):
         return pltpu.make_async_remote_copy(
-            src_ref=gathered.at[slot, me],
-            dst_ref=gathered.at[slot, me],
-            send_sem=send_sem.at[slot, d],
-            recv_sem=recv_sem.at[slot, d],
-            device_id={"space": peer},
+            src_ref=gathered.at[slot, what],
+            dst_ref=gathered.at[slot, what],
+            send_sem=send_sem.at[slot, sem],
+            recv_sem=recv_sem.at[slot, what],
+            device_id={"space": where},
             device_id_type=MESH,
         )
 
-    def copy_from(slot, d):
-        peer = lax.rem(me + spaces - d, spaces)
-        return peer, pltpu.make_async_remote_copy(
-            src_ref=gathered.at[slot, me],
-            dst_ref=gathered.at[slot, peer],
-            send_sem=send_sem.at[slot, d],
-            recv_sem=recv_sem.at[slot, d],
-            device_id={"space": peer},
-            device_id_type=MESH,
-        )
+    order = sorted(range(1, chips), key=lambda d: (-(d % 2) - (d // 2), d))
+
+    def mirror(p):
+        return p + 1 - 2 * core
+
+    def sends(slot):
+        found = [copy(slot, me, twin(d, 1), d) for d in order]
+        found += [copy(slot, me, mirror(twin(d, 1)), chips + d) for d in order]
+        return found + [copy(slot, me, partner, 0)]
 
     def pass_copy():
         return pltpu.make_async_remote_copy(
@@ -195,18 +205,23 @@
         lax.fori_loop(0, blocks // per, body, 0)
 
     def evaluate(slot):
-        for d in range(1, spaces):
-            copy_to(slot, d).start()
+        for each in sends(slot):
+            each.start()
         target_features(slot)
         source_features(slot, me)
 
-        def arrive(d, carry):
-            peer, copy = copy_from(slot, d)
-            copy.wait_recv()
-            source_features(slot, peer)
-            return carry
-
-        lax.fori_loop(1, spaces, arrive, 0)
+        def arrived(p):
+            copy(slot, p, p, 0).wait_recv()
+
+        near = order[::-1]
+        arrived(partner)
+        source_features(slot, partner)
+        for d in near:
+            arrived(twin(d, -1))
+            source_features(slot, twin(d, -1))
+        for d in near:
+            arrived(mirror(twin(d, -1)))
+            source_features(slot, mirror(twin(d, -1)))
         all_targets()
         x = [gathered[slot, me, r] for r in range(3)]
         a = [gathered[slot, me, 3 + r] for r in range(3)]
@@ -221,8 +236,8 @@
         for r in range(3):
             rate[r] = -inv_four_pi * (cross_v[r] - three_b[r])
             rate[3 + r] = -inv_four_pi * (cross_s[r] - 3.0 * (cross_f[r] - five_b[r]))
-        for d in range(1, spaces):
-            copy_to(slot, d).wait_send()
+        for each in sends(slot):
+            each.wait_send()
 
     def write_out(value):
         for b in range(blocks):
@@ -292,9 +307,9 @@
         @pl.when(part == 4)
         def _():
             outgoing[...] = current + h * now
-            copy = pass_copy()
-            copy.start()
-            copy.wait_send()
+            handed = pass_copy()
+            handed.start()
+            handed.wait_send()
 
         return carry
 

time: 85.5 us -> 81.1 us (0.949)
  Pallas kernels: 83.8 us -> 79.4 us
    pallas_call x1, Pallas kernels: 83.8 us -> 79.4 us  [per_device(): pl.pallas_call(functools.partial(kernel, spaces, slices, blocks, width),...]
where the time goes in v2:
time: 81.1 us; the launch traced here: 80.8 us
  Pallas kernels  79.4 us (98%)
  local copies, waits for them, and re-layouts  1.39 us (2%)
    pallas_call x1, Pallas kernels, per_device(): pl.pallas_call(functools.partial(kernel, spaces, slices, blocks, width),...  79.4 us

profile of v2, /device:TPU:24, one launch (start us, length us, event | category | flops | bytes accessed | tf_op | source)
XLA Modules:
  0.0 80.8 jit_solution(1870253760993987431)
XLA Ops:
  0.0 79.4 %shard_map.46 = f32[1,6,1024]{2,1,0:T(8,128)} custom-call(f32[3,1024]{1,0:T(4,128)} %pos_ref.1, f32[3,1024]{1,0:T(4,128)} %str_ref.1, s32[8,8]{1,0:T(8,128)} %list_ref.1, s32[64]{0:T(128)} %slot_ref.1), custom_call_target="tpu_custom_call" | custom-call | tf_op jit(solution)/shard_map/pallas_call | solution.py:325
  79.5 1.4 %copy.5 = f32[1,6,1024]{2,0,1:T(1,128)} copy(f32[1,6,1024]{2,1,0:T(8,128)} %shard_map.46) | data formatting | bytes 49152 | tf_op jit(solution)/shard_map/pallas_call | solution.py:325
